TPU v7x, 512 devices: a whole 4x4x16 slice. The times are simulated.
512 devices in a mesh: dp: 4 (over y), expert: 128 (over x, z, core).
Axes of the slice: x: 4, y: 4, z: 16, core: 2. Of those that a mesh axis runs over, the one named last changes fastest.
Arguments:
- tokens: bfloat16 [16384, 2048], P('expert', 'dp'), may hold values from -6 to 6
- routes: int32 [16384, 2], P('expert'), may hold values from 0 to 127, all different within a row; in each aligned block of 128 rows (0 to 127, 128 to 255, ...) at most 3 rows name the same one
- route_weights: float32 [16384, 2], P('expert'), may hold values from 0.02 to 0.3
- live_tokens: int32 [128], P('expert'), may hold values from 33 to 128, as said below
- gate_codes: bfloat16 [2048, 98304], P('dp', 'expert'), may hold values from -4 to 4
- gate_scales: float32 [16, 768], P('dp', 'expert'), may hold values from 0.011 to 0.044
- up_codes: bfloat16 [2048, 98304], P('dp', 'expert'), may hold values from -4 to 4
- up_scales: float32 [16, 768], P('dp', 'expert'), may hold values from 0.011 to 0.044
- down_codes: bfloat16 [98304, 2048], P('expert', 'dp'), may hold values from -4 to 4
- down_scales: float32 [768, 16], P('expert', 'dp'), may hold values from 0.018 to 0.072
- grad_out: bfloat16 [16384, 2048], P('expert', 'dp'), may hold values from -6 to 6
Outputs:
- grad_tokens: bfloat16 [16384, 2048], P('expert', 'dp')
- grad_route_weights: float32 [16384, 2], P('expert')
- grad_gate_proj: bfloat16 [2048, 98304], P('dp', 'expert')
- grad_up_proj: bfloat16 [2048, 98304], P('dp', 'expert')
- grad_down_proj: bfloat16 [98304, 2048], P('expert', 'dp')
Inputs may be any that keep to these rules, and one draw needn't show every extreme that they name: `routes`: in every aligned block of 128 rows (the tokens of one group) each row names 2 different experts, and no expert is named by more than 3 rows of the block; some expert is named by exactly 3 rows of some block. `live_tokens`: some group is full and some group holds the fewest live tokens.
All inputs are finite; a program needn't handle non-finite values.
Results may differ from a plain program's by a relative error of at most 0.023.
Values may be sent and summed in bfloat16 or wider, within the bound.
No kernel may reach another device: no remote copies, remote signals or barrier semaphores. Data moves between devices by JAX's collectives and lax.ppermute only.
A program may use at most 64 MiB of HBM per device.

v0:
```python
import jax
import jax.numpy as jnp
from jax import lax
from jax.experimental import pallas as pl
from jax.experimental.pallas import tpu as pltpu
from jax.sharding import PartitionSpec as P


BF = jnp.bfloat16
F32 = jnp.float32
CAP = 3
LANES = 128
GRANT = 62 << 20
MIDDLE = 50 << 20
SMALL = 24 << 20
LAST = (((1,), (1,)), ((), ()))
FIRST = (((0,), (0,)), ((), ()))
VMEM = pl.BlockSpec(memory_space=pltpu.VMEM)
SMEM = pl.BlockSpec(memory_space=pltpu.SMEM)
ANY = pl.BlockSpec(memory_space=pl.ANY)


def split3(v):
    hi = v.astype(BF)
    rest = v - hi.astype(F32)
    mid = rest.astype(BF)
    lo = (rest - mid.astype(F32)).astype(BF)
    return hi, mid, lo


def call(kernel, outs, in_specs, args, flops=0, nbytes=0, scratch=(), grant=GRANT):
    return pl.pallas_call(
        kernel,
        out_shape=outs,
        in_specs=in_specs,
        out_specs=jax.tree.map(lambda _: VMEM, outs),
        scratch_shapes=scratch,
        compiler_params=pltpu.CompilerParams(vmem_limit_bytes=grant),
        cost_estimate=pl.CostEstimate(flops=flops, bytes_accessed=nbytes, transcendentals=0),
    )(*args)


def slot_kernel(live_ref, routes_ref, weights_ref, tokens_ref, grad_ref, send_ref, slots_ref, mix_ref):
    count, quarter = tokens_ref.shape
    experts = slots_ref.shape[0] // CAP
    wide = quarter // LANES
    chunks = 2 * CAP * wide
    expert = lax.broadcasted_iota(jnp.int32, (experts, count), 0)
    live = lax.broadcasted_iota(jnp.int32, (experts, count), 1) < live_ref[0]
    first = (routes_ref[0:1, :] == expert) & live
    second = (routes_ref[1:2, :] == expert) & live
    member = first | second
    before = (
        lax.broadcasted_iota(jnp.int32, (count, count), 0)
        < lax.broadcasted_iota(jnp.int32, (count, count), 1)
    ).astype(BF)
    ahead = jnp.dot(member.astype(BF), before, preferred_element_type=F32)
    weight = jnp.where(first, weights_ref[0:1, :], weights_ref[1:2, :])
    for p in range(CAP):
        chosen = member & (ahead == float(p))
        one_hot = chosen.astype(BF)
        slots_ref[p * experts : (p + 1) * experts, :] = one_hot
        picked = jnp.dot(one_hot, tokens_ref[...], preferred_element_type=F32)
        scaled = jnp.zeros((experts, quarter), F32)
        for piece in split3(jnp.where(chosen, weight, 0.0)):
            scaled = scaled + jnp.dot(piece, grad_ref[...], preferred_element_type=F32)
        for kind, value in enumerate((picked, scaled)):
            for h in range(wide):
                at = (kind * CAP + p) * wide + h
                mix_ref[pl.ds(at, experts, stride=chunks), :] = value[:, h * LANES : (h + 1) * LANES]
    send_ref[...] = mix_ref[...].astype(BF)


def dequant(scale_ref, code_ref, out_ref, base):
    for i in range(scale_ref.shape[0]):
        for j in range(scale_ref.shape[1]):
            lines = slice(i * LANES, (i + 1) * LANES)
            lanes = slice(j * LANES, (j + 1) * LANES)
            out_ref[base + i * LANES : base + (i + 1) * LANES, lanes] = (
                code_ref[lines, lanes].astype(F32) * scale_ref[i, j]
            ).astype(BF)


def dequant_pair_kernel(gs_ref, us_ref, gc_ref, uc_ref, out_ref):
    dequant(gs_ref, gc_ref, out_ref, 0)
    dequant(us_ref, uc_ref, out_ref, gc_ref.shape[0])


def dequant_one_kernel(ds_ref, dc_ref, out_ref):
    dequant(ds_ref, dc_ref, out_ref, 0)


def unpack(got_ref, mix_ref, rows_ref, parts):
    slots, width = rows_ref.shape
    groups = slots // CAP
    near = groups // parts
    chunks = CAP * width // LANES
    wide = width // (2 * LANES)
    mix_ref[...] = got_ref[...].astype(F32)
    for kind in range(2):
        for p in range(CAP):
            for h in range(wide):
                at = (kind * CAP + p) * wide + h
                lane = (kind * wide + h) * LANES
                value = mix_ref[pl.ds(at, groups, stride=chunks), :].astype(BF)
                for j in range(parts):
                    line = (j * CAP + p) * near
                    rows_ref[line : line + near, lane : lane + LANES] = value[
                        j * near : (j + 1) * near
                    ]


def row_kernel(got_ref, wd_ref, out_ref, rows_ref, mix_ref):
    parts, span, _ = out_ref.shape
    quarter = rows_ref.shape[1] // 2
    unpack(got_ref, mix_ref, rows_ref, parts)
    back = lax.dot_general(
        rows_ref[:, quarter:], wd_ref[...], LAST, preferred_element_type=F32
    ).astype(BF)
    for j in range(parts):
        lines = slice(j * span, (j + 1) * span)
        out_ref[j, :, :quarter] = rows_ref[lines, :quarter]
        out_ref[j, :, quarter:] = back[lines]


def act_kernel(
    me_ref, part_ref, own_hbm, next_hbm, far_low_hbm, far_high_hbm, prev_hbm, out_ref, act_ref, w_ref, mix_ref, sems
):
    parts, span, _ = part_ref.shape
    near = span // CAP
    quarter = w_ref.shape[1] // 2
    wide = quarter // LANES
    chunks = out_ref.shape[1] // near
    owners = [lax.rem(me_ref[0] + shift, parts) for shift in range(parts)]
    copies = [
        pltpu.make_async_copy(source, target, sems.at[n])
        for n, (source, target) in enumerate(
            (
                (own_hbm, w_ref.at[0]),
                (next_hbm, w_ref.at[1]),
                (prev_hbm, w_ref.at[3]),
                (far_low_hbm, w_ref.at[2, :quarter]),
                (far_high_hbm, w_ref.at[2, quarter:]),
            )
        )
    ]
    for copy in copies:
        copy.start()
    grad_hidden = part_ref[0, :, quarter:].astype(F32)
    for j in range(1, parts):
        grad_hidden = grad_hidden + part_ref[j, :, quarter:].astype(F32)
    gate_pre = up_pre = 0.0
    for shift, needed in ((0, (0,)), (1, (1,)), (3, (2,)), (2, (3, 4))):
        for n in needed:
            copies[n].wait()
        token_rows = part_ref[owners[shift], :, :quarter]
        gate = jnp.dot(token_rows, w_ref[shift, :quarter, :], preferred_element_type=F32)
        gate_pre = gate_pre + gate.astype(BF).astype(F32)
        up = jnp.dot(token_rows, w_ref[shift, quarter:, :], preferred_element_type=F32)
        up_pre = up_pre + up.astype(BF).astype(F32)
    sig = jax.nn.sigmoid(gate_pre)
    activated = gate_pre * sig
    hidden = (activated * up_pre).astype(BF)
    gate_delta = (grad_hidden * up_pre * sig * (1.0 + gate_pre * (1.0 - sig))).astype(BF)
    up_delta = (grad_hidden * activated).astype(BF)
    act_ref[0:span, :] = gate_delta
    act_ref[span : 2 * span, :] = up_delta
    act_ref[2 * span : 3 * span, :] = hidden
    score = jnp.sum(hidden.astype(F32) * grad_hidden, axis=1, keepdims=True)
    lane = lax.broadcasted_iota(jnp.int32, (span, LANES), 1)
    hi, mid, lo = (v.astype(F32) for v in split3(score))
    scores = jnp.where(lane == 0, hi, jnp.where(lane == 1, mid, jnp.where(lane == 2, lo, 0.0)))
    for p in range(CAP):
        mix_ref[pl.ds(CAP * wide + p, near, stride=chunks), :] = scores[p * near : (p + 1) * near]
    for c in range(CAP * wide + CAP, chunks):
        mix_ref[pl.ds(c, near, stride=chunks), :] = jnp.zeros((near, LANES), F32)
    for shift in range(parts):
        grad = lax.dot_general(
            gate_delta, w_ref[shift, :quarter, :], LAST, preferred_element_type=F32
        )
        grad = grad + lax.dot_general(
            up_delta, w_ref[shift, quarter:, :], LAST, preferred_element_type=F32
        )
        for p in range(CAP):
            for h in range(wide):
                mix_ref[pl.ds(p * wide + h, near, stride=chunks), :] = grad[
                    p * near : (p + 1) * near, h * LANES : (h + 1) * LANES
                ]
        out_ref[owners[shift]] = mix_ref[...].astype(BF)


def weight_grad_kernel(
    me_ref, got_ref, a0_ref, a1_ref, a2_ref, a3_ref, gg_ref, gu_ref, gd_ref, rows_ref, mix_ref
):
    parts = 4
    unpack(got_ref, mix_ref, rows_ref, parts)
    span = a0_ref.shape[0] // 3
    quarter = gg_ref.shape[0]
    rows, acts = [], []
    for shift, ref in enumerate((a0_ref, a1_ref, a2_ref, a3_ref)):
        owner = lax.rem(me_ref[0] + parts - shift, parts)
        rows.append(rows_ref[pl.ds(pl.multiple_of(owner * span, span), span), :])
        acts.append(ref)
    rows = jnp.concatenate(rows, axis=0)

    def gathered(k):
        return jnp.concatenate([ref[k * span : (k + 1) * span, :] for ref in acts], axis=0)

    token_rows = rows[:, :quarter]
    gg_ref[...] = lax.dot_general(
        token_rows, gathered(0), FIRST, preferred_element_type=F32
    ).astype(BF)
    gu_ref[...] = lax.dot_general(
        token_rows, gathered(1), FIRST, preferred_element_type=F32
    ).astype(BF)
    gd_ref[...] = lax.dot_general(
        gathered(2), rows[:, quarter:], FIRST, preferred_element_type=F32
    ).astype(BF)


def home_kernel(routes_ref, weights_ref, slots_ref, ret_ref, grad_ref, score_ref, mix_ref):
    slots, count = slots_ref.shape
    experts = slots // CAP
    quarter = grad_ref.shape[1]
    wide = quarter // LANES
    chunks = ret_ref.shape[0] // experts
    mix_ref[...] = ret_ref[...].astype(F32)

    def chunk(c):
        return mix_ref[pl.ds(c, experts, stride=chunks), :]

    grad = jnp.zeros((count, quarter), F32)
    expert = lax.broadcasted_iota(jnp.int32, (experts, count), 0)
    scores = [jnp.zeros((1, count), F32)] * 2
    for p in range(CAP):
        one_hot = slots_ref[p * experts : (p + 1) * experts, :]
        block = jnp.concatenate([chunk(p * wide + h).astype(BF) for h in range(wide)], axis=1)
        grad = grad + lax.dot_general(one_hot, block, FIRST, preferred_element_type=F32)
        pieces = chunk(CAP * wide + p)
        picked = one_hot.astype(F32) * (pieces[:, 0:1] + pieces[:, 1:2] + pieces[:, 2:3])
        for k in range(2):
            mine = jnp.where(routes_ref[k : k + 1, :] == expert, picked, 0.0)
            scores[k] = scores[k] + jnp.sum(mine, axis=0, keepdims=True)
    grad_ref[...] = grad.astype(BF)
    for k in range(2):
        score_ref[k : k + 1, :] = scores[k] / weights_ref[k : k + 1, :]


def layer(
    tokens,
    routes,
    route_weights,
    live_tokens,
    gate_codes,
    gate_scales,
    up_codes,
    up_scales,
    down_codes,
    down_scales,
    grad_out,
):
    count, quarter = tokens.shape
    hidden_size = gate_codes.shape[1]
    experts = lax.axis_size("expert")
    parts = lax.axis_size("dp")
    slots = experts * CAP
    span = slots // parts
    shape = jax.ShapeDtypeStruct
    routes_t = routes.T
    weights_t = route_weights.T

    wide = quarter // LANES
    out_chunks = 2 * CAP * wide
    back_chunks = -(-(CAP * wide + CAP) // 8) * 8
    me = lax.axis_index("dp")

    def turn(value, shift):
        return lax.ppermute(value, "dp", [(i, (i + shift) % parts) for i in range(parts)])

    w_own = call(
        dequant_pair_kernel,
        shape((2 * quarter, hidden_size), BF),
        [SMEM] * 2 + [VMEM] * 2,
        (gate_scales, up_scales, gate_codes, up_codes),
        flops=2 * quarter * hidden_size,
        nbytes=8 * quarter * hidden_size,
    )
    w_prev = turn(w_own, 1)
    w_next = turn(w_own, -1)
    send, one_hot = call(
        slot_kernel,
        (shape((experts * out_chunks, LANES), BF), shape((slots, count), BF)),
        [SMEM, VMEM, VMEM, VMEM, VMEM],
        (live_tokens, routes_t, weights_t, tokens, grad_out),
        grant=SMALL,
        flops=2 * slots * count * quarter * 4,
        nbytes=2 * slots * 2 * quarter,
        scratch=[pltpu.VMEM((experts * out_chunks, LANES), F32)],
    )
    got = lax.all_to_all(
        send.reshape(experts, out_chunks, LANES),
        "expert",
        split_axis=0,
        concat_axis=0,
        tiled=True,
    )
    far_low = turn(w_next[:quarter], -1)
    far_high = turn(w_prev[quarter:], 1)
    w_down = call(
        dequant_one_kernel,
        shape(down_codes.shape, BF),
        [SMEM, VMEM],
        (down_scales, down_codes),
        grant=MIDDLE,
        flops=quarter * hidden_size,
        nbytes=4 * quarter * hidden_size,
    )
    got = got.reshape(experts * out_chunks, LANES)
    unpacking = [
        pltpu.VMEM((slots, 2 * quarter), BF),
        pltpu.VMEM((experts * out_chunks, LANES), F32),
    ]
    part = call(
        row_kernel,
        shape((parts, span, quarter + hidden_size), BF),
        [VMEM] * 2,
        (got, w_down),
        grant=MIDDLE,
        flops=2 * slots * quarter * hidden_size,
        nbytes=8 * slots * hidden_size,
        scratch=unpacking,
    )
    part = lax.all_to_all(part, "dp", split_axis=0, concat_axis=0, tiled=True)
    ret, acts = call(
        act_kernel,
        (
            shape((parts, span // CAP * back_chunks, LANES), BF),
            shape((3 * span, hidden_size), BF),
        ),
        [SMEM, VMEM] + [ANY] * 5,
        (me.reshape(1), part, w_own, w_next, far_low, far_high, w_prev),
        grant=MIDDLE,
        flops=8 * slots * quarter * hidden_size,
        nbytes=16 * quarter * hidden_size,
        scratch=[
            pltpu.VMEM((parts, 2 * quarter, hidden_size), BF),
            pltpu.VMEM((span // CAP * back_chunks, LANES), F32),
            pltpu.SemaphoreType.DMA((5,)),
        ],
    )
    ret = lax.all_to_all(ret, "dp", split_axis=0, concat_axis=0, tiled=True)
    ret, acts = lax.optimization_barrier((ret, acts))
    ret = lax.all_to_all(
        ret.reshape(experts, back_chunks, LANES), "expert", split_axis=0, concat_axis=0, tiled=True
    )
    grad_gate, grad_up, grad_down = call(
        weight_grad_kernel,
        (
            shape((quarter, hidden_size), BF),
            shape((quarter, hidden_size), BF),
            shape((hidden_size, quarter), BF),
        ),
        [SMEM] + [VMEM] * 5,
        (me.reshape(1), got, acts, turn(acts, 1), turn(acts, 2), turn(acts, 3)),
        grant=SMALL,
        flops=6 * slots * quarter * hidden_size,
        nbytes=16 * slots * hidden_size,
        scratch=unpacking,
    )
    grad_tokens, grad_weights_t = call(
        home_kernel,
        (shape((count, quarter), BF), shape((2, count), F32)),
        [VMEM] * 4,
        (routes_t, weights_t, one_hot, ret.reshape(experts * back_chunks, LANES)),
        grant=SMALL,
        flops=2 * slots * count * quarter,
        nbytes=2 * slots * quarter,
        scratch=[pltpu.VMEM((experts * back_chunks, LANES), F32)],
    )
    return (grad_tokens, grad_weights_t.T, grad_gate, grad_up, grad_down)


def solution(mesh):
    placed = (
        P("expert", "dp"),
        P("expert", None),
        P("expert", None),
        P("expert"),
        P("dp", "expert"),
        P("dp", "expert"),
        P("dp", "expert"),
        P("dp", "expert"),
        P("expert", "dp"),
        P("expert", "dp"),
        P("expert", "dp"),
    )
    return jax.shard_map(
        layer,
        mesh=mesh,
        in_specs=placed,
        out_specs=(
            P("expert", "dp"),
            P("expert", None),
            P("dp", "expert"),
            P("dp", "expert"),
            P("expert", "dp"),
        ),
        check_vma=False,
    )
```

profile of v0, /device:TPU:1, one launch (start us, length us, event | category | flops | bytes accessed | tf_op | source)
XLA Modules:
  0.0 173.4 jit_solution(2054755589088569178)
XLA Ops:
  1.3 0.0 copy-start.1
  1.3 0.7 copy-done.1
  2.0 0.7 copy-done.3
  2.6 0.9 copy-done.7
  3.5 0.9 copy-done.8
  4.4 1.7 shard_map.146
  6.1 20.4 %all-to-all-start = ((bf16[128,24,128]{2,1,0:T(8,128)(2,1)}), bf16[128,24,128]{2,1,0:T(8,128)(2,1)S(1)}, u32[]{:S(2)}, u32[]{:S(2)}) async-start(bf16[128,24,128]{2,1,0:T(8,128)(2,1)} %bitcast.3), calls=%async_computation | async-start | bytes 1572864 | tf_op jit(solution)/shard_map/all_to_all | solution.py:300
  26.5 2.9 %shard_map.149.own_hbm = bf16[1024,768]{1,0:T(8,128)(2,1)} custom-call(f32[4,6]{1,0:T(4,128)} %gs_ref.1, f32[4,6]{1,0:T(4,128)} %us_ref.1, bf16[512,768]{1,0:T(8,128)(2,1)} %gc_ref.1, bf16[512,768]{1,0:T(8,128)(2,1)} %uc_ref.1), custom_call_target="tpu_custom_call" | custom-call | flops 786432 | bytes 3145728 | tf_op jit(solution)/shard_map/pallas_call | solution.py:32
  29.4 3.3 %collective-permute-start.2 = (bf16[1024,768]{1,0:T(8,128)(2,1)}, bf16[1024,768]{1,0:T(8,128)(2,1)S(1)}, u32[]{:S(2)}, u32[]{:S(2)}) collective-permute-start(bf16[1024,768]{1,0:T(8,128)(2,1)} %shard_map.149.own_hbm), channel_id=1, source_target_pairs={{0,128},{128,256},{256,384},{384,0},{1,129},{129,257},{257,385},{3... | collective-permute-start | bytes 4718600 | tf_op jit(solution)/shard_map/ppermute | solution.py:278
  32.7 3.4 %collective-permute-start = (bf16[1024,768]{1,0:T(8,128)(2,1)}, bf16[1024,768]{1,0:T(8,128)(2,1)S(1)}, u32[]{:S(2)}, u32[]{:S(2)}) collective-permute-start(bf16[1024,768]{1,0:T(8,128)(2,1)} %shard_map.149.own_hbm), channel_id=1, source_target_pairs={{0,384},{128,0},{256,128},{384,256},{1,385},{129,1},{257,129},{385... | collective-permute-start | bytes 4718600 | tf_op jit(solution)/shard_map/ppermute | solution.py:278
  36.1 31.9 %collective-permute-done.2.prev_hbm = bf16[1024,768]{1,0:T(8,128)(2,1)S(1)} collective-permute-done((bf16[1024,768]{1,0:T(8,128)(2,1)}, bf16[1024,768]{1,0:T(8,128)(2,1)S(1)}, u32[]{:S(2)}, u32[]{:S(2)}) %collective-permute-start.2) | collective-permute-done | bytes 1572896 | tf_op jit(solution)/shard_map/ppermute | solution.py:278
  68.0 0.1 slice.9
  68.1 1.9 %collective-permute-start.3 = (bf16[512,768]{1,0:T(8,128)(2,1)S(1)}, bf16[512,768]{1,0:T(8,128)(2,1)S(1)}, u32[]{:S(2)}, u32[]{:S(2)}) collective-permute-start(bf16[512,768]{1,0:T(8,128)(2,1)S(1)} %slice.9), channel_id=1, source_target_pairs={{0,128},{128,256},{256,384},{384,0},{1,129},{129,257},{257,385},{3... | collective-permute-start | bytes 2359304 | tf_op jit(solution)/shard_map/ppermute | solution.py:278
  70.0 0.0 collective-permute-done.next_hbm
  70.0 0.0 copy-start.10
  70.0 1.0 slice.8
  71.0 0.0 copy-done.9
  71.0 0.4 copy-done.10
  71.5 4.6 %collective-permute-start.1 = (bf16[512,768]{1,0:T(8,128)(2,1)}, bf16[512,768]{1,0:T(8,128)(2,1)}, u32[]{:S(2)}, u32[]{:S(2)}) collective-permute-start(bf16[512,768]{1,0:T(8,128)(2,1)} %slice.8), channel_id=1, source_target_pairs={{0,384},{128,0},{256,128},{384,256},{1,385},{129,1},{257,129},{385... | collective-permute-start | bytes 2359304 | tf_op jit(solution)/shard_map/ppermute | solution.py:278
  76.0 0.0 copy-done.11
  76.0 0.1 copy.16.ds_ref
  76.1 1.1 copy-done
  77.3 0.8 shard_map.147.wd_ref
  78.0 0.0 all-to-all-done
  78.0 1.8 %shard_map.148 = bf16[4,96,1280]{2,1,0:T(8,128)(2,1)} custom-call(bf16[3072,128]{1,0:T(8,128)(2,1)S(1)} %bitcast.8, bf16[768,512]{1,0:T(8,128)(2,1)S(1)} %shard_map.147.wd_ref), custom_call_target="tpu_custom_call" | custom-call | flops 301989888 | bytes 2359296 | tf_op jit(solution)/shard_map/pallas_call | solution.py:32
  79.9 3.5 %all-to-all-start.1 = ((bf16[4,96,1280]{2,1,0:T(8,128)(2,1)}), bf16[4,96,1280]{2,1,0:T(8,128)(2,1)S(1)}, u32[]{:S(2)}, u32[]{:S(2)}) async-start(bf16[4,96,1280]{2,1,0:T(8,128)(2,1)} %shard_map.148), calls=%async_computation.1 | async-start | bytes 1966080 | tf_op jit(solution)/shard_map/all_to_all | solution.py:333
  83.4 5.2 %collective-permute-done.3.far_high_hbm = bf16[512,768]{1,0:T(8,128)(2,1)S(1)} collective-permute-done((bf16[512,768]{1,0:T(8,128)(2,1)S(1)}, bf16[512,768]{1,0:T(8,128)(2,1)S(1)}, u32[]{:S(2)}, u32[]{:S(2)}) %collective-permute-start.3) | collective-permute-done | bytes 786464 | tf_op jit(solution)/shard_map/ppermute | solution.py:278
  88.6 2.7 %collective-permute-done.1.far_low_hbm = bf16[512,768]{1,0:T(8,128)(2,1)} collective-permute-done((bf16[512,768]{1,0:T(8,128)(2,1)}, bf16[512,768]{1,0:T(8,128)(2,1)}, u32[]{:S(2)}, u32[]{:S(2)}) %collective-permute-start.1) | collective-permute-done | bytes 786464 | tf_op jit(solution)/shard_map/ppermute | solution.py:278
  91.3 7.7 %all-to-all-done.1.part_ref = bf16[4,96,1280]{2,1,0:T(8,128)(2,1)S(1)} async-done(((bf16[4,96,1280]{2,1,0:T(8,128)(2,1)}), bf16[4,96,1280]{2,1,0:T(8,128)(2,1)S(1)}, u32[]{:S(2)}, u32[]{:S(2)}) %all-to-all-start.1) | async-done | bytes 983072 | tf_op jit(solution)/shard_map/all_to_all | solution.py:333
  98.9 5.2 %shard_map.150 = (bf16[4,512,128]{2,1,0:T(8,128)(2,1)S(1)}, bf16[288,768]{1,0:T(8,128)(2,1)S(1)}) custom-call(s32[1]{0:T(128)} %bitcast.2.me_ref, bf16[4,96,1280]{2,1,0:T(8,128)(2,1)S(1)} %all-to-all-done.1.part_ref, bf16[1024,768]{1,0:T(8,128)(2,1)} %shard_map.149.own_hbm, bf16[1024,768]{1,0:T(8,128)(2,1)} %copy-done.10, ...), custom_call_target="tpu_custom_call" | custom-call | flops 1207959552 | bytes 6291456 | tf_op jit(solution)/shard_map/pallas_call | solution.py:32
  104.2 0.0 copy-start.5
  104.2 12.8 %all_to_all.20 = bf16[4,512,128]{2,1,0:T(8,128)(2,1)} all-to-all(bf16[4,512,128]{2,1,0:T(8,128)(2,1)S(1)} %get-tuple-element.18), channel_id=1, replica_groups=mesh['dp'=4,'expert'=128] {'dp'}, dimensions={0} | all-to-all | bytes 1048576 | tf_op jit(solution)/shard_map/all_to_all | solution.py:351
  117.0 0.0 copy-done.5
  117.0 22.0 %all-to-all-start.3 = ((bf16[128,16,128]{2,1,0:T(8,128)(2,1)}), bf16[128,16,128]{2,1,0:T(8,128)(2,1)S(1)}, u32[]{:S(2)}, u32[]{:S(2)}) async-start(bf16[128,16,128]{2,1,0:T(8,128)(2,1)} %bitcast.5), calls=%async_computation.3 | async-start | bytes 1048576 | tf_op jit(solution)/shard_map/all_to_all | solution.py:353
  139.0 0.0 copy-start.2
  139.0 0.0 copy-start.4
  139.0 2.8 %collective-permute-start.6 = (bf16[288,768]{1,0:T(8,128)(2,1)}, bf16[288,768]{1,0:T(8,128)(2,1)S(1)}, u32[]{:S(2)}, u32[]{:S(2)}) collective-permute-start(bf16[288,768]{1,0:T(8,128)(2,1)} %copy-done.5), channel_id=1, source_target_pairs={{0,384},{128,0},{256,128},{384,256},{1,385},{129,1},{257,129},{385... | collective-permute-start | bytes 1327112 | tf_op jit(solution)/shard_map/ppermute | solution.py:278
  141.8 3.1 %collective-permute-start.5 = (bf16[288,768]{1,0:T(8,128)(2,1)}, bf16[288,768]{1,0:T(8,128)(2,1)S(1)}, u32[]{:S(2)}, u32[]{:S(2)}) collective-permute-start(bf16[288,768]{1,0:T(8,128)(2,1)} %copy-done.5), channel_id=1, source_target_pairs={{0,256},{128,384},{256,0},{384,128},{1,257},{129,385},{257,1},{385... | collective-permute-start | bytes 1327112 | tf_op jit(solution)/shard_map/ppermute | solution.py:278
  144.9 1.9 %collective-permute-start.4 = (bf16[288,768]{1,0:T(8,128)(2,1)}, bf16[288,768]{1,0:T(8,128)(2,1)S(1)}, u32[]{:S(2)}, u32[]{:S(2)}) collective-permute-start(bf16[288,768]{1,0:T(8,128)(2,1)} %copy-done.5), channel_id=1, source_target_pairs={{0,128},{128,256},{256,384},{384,0},{1,129},{129,257},{257,385},{3... | collective-permute-start | bytes 1327112 | tf_op jit(solution)/shard_map/ppermute | solution.py:278
  146.9 5.1 %collective-permute-done.6.a3_ref = bf16[288,768]{1,0:T(8,128)(2,1)S(1)} collective-permute-done((bf16[288,768]{1,0:T(8,128)(2,1)}, bf16[288,768]{1,0:T(8,128)(2,1)S(1)}, u32[]{:S(2)}, u32[]{:S(2)}) %collective-permute-start.6) | collective-permute-done | bytes 442400 | tf_op jit(solution)/shard_map/ppermute | solution.py:278
  152.0 4.1 %collective-permute-done.5.a2_ref = bf16[288,768]{1,0:T(8,128)(2,1)S(1)} collective-permute-done((bf16[288,768]{1,0:T(8,128)(2,1)}, bf16[288,768]{1,0:T(8,128)(2,1)S(1)}, u32[]{:S(2)}, u32[]{:S(2)}) %collective-permute-start.5) | collective-permute-done | bytes 442400 | tf_op jit(solution)/shard_map/ppermute | solution.py:278
  156.1 11.0 %collective-permute-done.4.a1_ref = bf16[288,768]{1,0:T(8,128)(2,1)S(1)} collective-permute-done((bf16[288,768]{1,0:T(8,128)(2,1)}, bf16[288,768]{1,0:T(8,128)(2,1)S(1)}, u32[]{:S(2)}, u32[]{:S(2)}) %collective-permute-start.4) | collective-permute-done | bytes 442400 | tf_op jit(solution)/shard_map/ppermute | solution.py:278
  167.0 1.0 copy-done.6
  168.0 2.6 %shard_map.152 = (bf16[512,768]{1,0:T(8,128)(2,1)}, bf16[512,768]{1,0:T(8,128)(2,1)}, bf16[768,512]{1,0:T(8,128)(2,1)}) custom-call(s32[1]{0:T(128)} %bitcast.2.me_ref, bf16[3072,128]{1,0:T(8,128)(2,1)S(1)} %bitcast.9, bf16[288,768]{1,0:T(8,128)(2,1)S(1)} %copy-done.6, bf16[288,768]{1,0:T(8,128)(2,1)S(1)} %collective-permute-done.4.a1_ref, ...), custom_call_target="tpu_custom_call" | custom-call | flops 905969664 | bytes 4718592 | tf_op jit(solution)/shard_map/pallas_call | solution.py:32
  170.7 1.6 all-to-all-done.3
  172.2 0.0 copy-done.2
  172.2 0.0 copy-done.4
  172.2 1.2 shard_map.151
  (7 shorter events, 0.0 us)
Async XLA Ops:
  1.3 0.7 copy-start.1
  2.0 0.7 copy-start.3
  2.6 0.9 copy-start.7
  3.5 0.9 copy-start.8
  6.1 71.9 %all-to-all-start = ((bf16[128,24,128]{2,1,0:T(8,128)(2,1)}), bf16[128,24,128]{2,1,0:T(8,128)(2,1)S(1)}, u32[]{:S(2)}, u32[]{:S(2)}) async-start(bf16[128,24,128]{2,1,0:T(8,128)(2,1)} %bitcast.3), calls=%async_computation | async-start | bytes 1572864 | tf_op jit(solution)/shard_map/all_to_all | solution.py:300
  29.4 46.7 %copy-start.11 = (f32[6,4]{0,1:T(4,128)S(1)}, f32[6,4]{0,1:T(4,128)}, u32[]{:S(2)}) copy-start(f32[6,4]{0,1:T(4,128)} %param.20) | copy-start | bytes 292
  29.4 38.6 %collective-permute-start.2 = (bf16[1024,768]{1,0:T(8,128)(2,1)}, bf16[1024,768]{1,0:T(8,128)(2,1)S(1)}, u32[]{:S(2)}, u32[]{:S(2)}) collective-permute-start(bf16[1024,768]{1,0:T(8,128)(2,1)} %shard_map.149.own_hbm), channel_id=1, source_target_pairs={{0,128},{128,256},{256,384},{384,0},{1,129},{129,257},{257,385},{3... | collective-permute-start | bytes 4718600 | tf_op jit(solution)/shard_map/ppermute | solution.py:278
  32.7 37.3 %collective-permute-start = (bf16[1024,768]{1,0:T(8,128)(2,1)}, bf16[1024,768]{1,0:T(8,128)(2,1)S(1)}, u32[]{:S(2)}, u32[]{:S(2)}) collective-permute-start(bf16[1024,768]{1,0:T(8,128)(2,1)} %shard_map.149.own_hbm), channel_id=1, source_target_pairs={{0,384},{128,0},{256,128},{384,256},{1,385},{129,1},{257,129},{385... | collective-permute-start | bytes 4718600 | tf_op jit(solution)/shard_map/ppermute | solution.py:278
  68.0 3.0 %copy-start.9 = (bf16[1024,768]{1,0:T(8,128)(2,1)}, bf16[1024,768]{1,0:T(8,128)(2,1)S(1)}, u32[]{:S(2)}) copy-start(bf16[1024,768]{1,0:T(8,128)(2,1)S(1)} %collective-permute-done.2.prev_hbm) | copy-start | bytes 4718596
  68.1 20.5 %collective-permute-start.3 = (bf16[512,768]{1,0:T(8,128)(2,1)S(1)}, bf16[512,768]{1,0:T(8,128)(2,1)S(1)}, u32[]{:S(2)}, u32[]{:S(2)}) collective-permute-start(bf16[512,768]{1,0:T(8,128)(2,1)S(1)} %slice.9), channel_id=1, source_target_pairs={{0,128},{128,256},{256,384},{384,0},{1,129},{129,257},{257,385},{3... | collective-permute-start | bytes 2359304 | tf_op jit(solution)/shard_map/ppermute | solution.py:278
  70.0 1.5 copy-start.10
  71.5 19.8 %collective-permute-start.1 = (bf16[512,768]{1,0:T(8,128)(2,1)}, bf16[512,768]{1,0:T(8,128)(2,1)}, u32[]{:S(2)}, u32[]{:S(2)}) collective-permute-start(bf16[512,768]{1,0:T(8,128)(2,1)} %slice.8), channel_id=1, source_target_pairs={{0,384},{128,0},{256,128},{384,256},{1,385},{129,1},{257,129},{385... | collective-permute-start | bytes 2359304 | tf_op jit(solution)/shard_map/ppermute | solution.py:278
  76.1 1.1 copy-start
  79.9 19.1 %all-to-all-start.1 = ((bf16[4,96,1280]{2,1,0:T(8,128)(2,1)}), bf16[4,96,1280]{2,1,0:T(8,128)(2,1)S(1)}, u32[]{:S(2)}, u32[]{:S(2)}) async-start(bf16[4,96,1280]{2,1,0:T(8,128)(2,1)} %shard_map.148), calls=%async_computation.1 | async-start | bytes 1966080 | tf_op jit(solution)/shard_map/all_to_all | solution.py:333
  104.2 12.8 %copy-start.5 = (bf16[288,768]{1,0:T(8,128)(2,1)}, bf16[288,768]{1,0:T(8,128)(2,1)S(1)}, u32[]{:S(2)}) copy-start(bf16[288,768]{1,0:T(8,128)(2,1)S(1)} %get-tuple-element.23.a0_ref) | copy-start | bytes 1327108
  117.0 55.2 %all-to-all-start.3 = ((bf16[128,16,128]{2,1,0:T(8,128)(2,1)}), bf16[128,16,128]{2,1,0:T(8,128)(2,1)S(1)}, u32[]{:S(2)}, u32[]{:S(2)}) async-start(bf16[128,16,128]{2,1,0:T(8,128)(2,1)} %bitcast.5), calls=%async_computation.3 | async-start | bytes 1048576 | tf_op jit(solution)/shard_map/all_to_all | solution.py:353
  139.0 33.2 %copy-start.2 = (s32[128,2]{0,1:T(2,128)S(1)}, s32[128,2]{0,1:T(2,128)}, u32[]{:S(2)}) copy-start(s32[128,2]{0,1:T(2,128)} %param.12) | copy-start | bytes 3076
  139.0 33.2 %copy-start.4 = (f32[128,2]{0,1:T(2,128)S(1)}, f32[128,2]{0,1:T(2,128)}, u32[]{:S(2)}) copy-start(f32[128,2]{0,1:T(2,128)} %param.13) | copy-start | bytes 3076
  139.0 12.9 %collective-permute-start.6 = (bf16[288,768]{1,0:T(8,128)(2,1)}, bf16[288,768]{1,0:T(8,128)(2,1)S(1)}, u32[]{:S(2)}, u32[]{:S(2)}) collective-permute-start(bf16[288,768]{1,0:T(8,128)(2,1)} %copy-done.5), channel_id=1, source_target_pairs={{0,384},{128,0},{256,128},{384,256},{1,385},{129,1},{257,129},{385... | collective-permute-start | bytes 1327112 | tf_op jit(solution)/shard_map/ppermute | solution.py:278
  141.8 14.2 %collective-permute-start.5 = (bf16[288,768]{1,0:T(8,128)(2,1)}, bf16[288,768]{1,0:T(8,128)(2,1)S(1)}, u32[]{:S(2)}, u32[]{:S(2)}) collective-permute-start(bf16[288,768]{1,0:T(8,128)(2,1)} %copy-done.5), channel_id=1, source_target_pairs={{0,256},{128,384},{256,0},{384,128},{1,257},{129,385},{257,1},{385... | collective-permute-start | bytes 1327112 | tf_op jit(solution)/shard_map/ppermute | solution.py:278
  144.9 22.1 %collective-permute-start.4 = (bf16[288,768]{1,0:T(8,128)(2,1)}, bf16[288,768]{1,0:T(8,128)(2,1)S(1)}, u32[]{:S(2)}, u32[]{:S(2)}) collective-permute-start(bf16[288,768]{1,0:T(8,128)(2,1)} %copy-done.5), channel_id=1, source_target_pairs={{0,128},{128,256},{256,384},{384,0},{1,129},{129,257},{257,385},{3... | collective-permute-start | bytes 1327112 | tf_op jit(solution)/shard_map/ppermute | solution.py:278
  167.0 1.0 copy-start.6
where the time goes:
time: 174 us; the launch traced here: 173 us
  waiting for transfers between devices  69.2 us (40%)
  starting transfers between devices  66.9 us (38%)
  Pallas kernels  16.1 us (9%)
  blocking collectives  12.8 us (7%)
  local copies, waits for them, and re-layouts  6.93 us (4%)
    ppermute x7, waiting for transfers between devices, turn(): lax.ppermute(value, 'dp', [(i, (i + shift) % parts) for i in range(parts)])  60 us
    all_to_all x1, starting transfers between devices, layer(): lax.all_to_all(ret.reshape(experts, back_chunks, LANES), 'expert', split_...  22 us
    ppermute x7, starting transfers between devices, turn(): lax.ppermute(value, 'dp', [(i, (i + shift) % parts) for i in range(parts)])  21 us
    all_to_all x1, starting transfers between devices, layer(): lax.all_to_all(send.reshape(experts, out_chunks, LANES), 'expert', split_...  20.4 us
    pallas_call x7, Pallas kernels, call(): pl.pallas_call(kernel, out_shape=outs, in_specs=in_specs, out_specs=jax.t...  16.1 us
    all_to_all x1, blocking collectives, layer(): ret = lax.all_to_all(ret, 'dp', split_axis=0, concat_axis=0, tiled=True)  12.8 us
    all_to_all x1, waiting for transfers between devices, layer(): part = lax.all_to_all(part, 'dp', split_axis=0, concat_axis=0, tiled=True)  7.67 us
    unnamed x25, local copies, waits for them, and re-layouts  5.87 us
  transfers between devices with their start and end apart: 10, of which 8 were waited for; matrix products, arithmetic and copies ran while one was open for 1% of the time, Pallas kernels for 5%

commit v1 on v0

--- a/solution.py
+++ b/solution.py
@@ -298,11 +298,7 @@
         scratch=[pltpu.VMEM((experts * out_chunks, LANES), F32)],
     )
     got = lax.all_to_all(
-        send.reshape(experts, out_chunks, LANES),
-        "expert",
-        split_axis=0,
-        concat_axis=0,
-        tiled=True,
+        send.reshape(experts, out_chunks, LANES), "expert", split_axis=0, concat_axis=0, tiled=True
     )
     far_low = turn(w_next[:quarter], -1)
     far_high = turn(w_prev[quarter:], 1)

time: 174 us -> 174 us (level)
  no operation moved by 1% of the time
where the time goes in v1:
time: 174 us; the launch traced here: 173 us
  waiting for transfers between devices  69.2 us (40%)
  starting transfers between devices  66.9 us (38%)
  Pallas kernels  16.1 us (9%)
  blocking collectives  12.8 us (7%)
  local copies, waits for them, and re-layouts  6.93 us (4%)
    ppermute x7, waiting for transfers between devices, turn(): lax.ppermute(value, 'dp', [(i, (i + shift) % parts) for i in range(parts)])  60 us
    all_to_all x1, starting transfers between devices, layer(): lax.all_to_all(ret.reshape(experts, back_chunks, LANES), 'expert', split_...  22 us
    ppermute x7, starting transfers between devices, turn(): lax.ppermute(value, 'dp', [(i, (i + shift) % parts) for i in range(parts)])  21 us
    all_to_all x1, starting transfers between devices, layer(): lax.all_to_all(send.reshape(experts, out_chunks, LANES), 'expert', split_...  20.4 us
    pallas_call x7, Pallas kernels, call(): pl.pallas_call(kernel, out_shape=outs, in_specs=in_specs, out_specs=jax.t...  16.1 us
    all_to_all x1, blocking collectives, layer(): ret = lax.all_to_all(ret, 'dp', split_axis=0, concat_axis=0, tiled=True)  12.8 us
    all_to_all x1, waiting for transfers between devices, layer(): part = lax.all_to_all(part, 'dp', split_axis=0, concat_axis=0, tiled=True)  7.67 us
    unnamed x25, local copies, waits for them, and re-layouts  5.87 us
  transfers between devices with their start and end apart: 10, of which 8 were waited for; matrix products, arithmetic and copies ran while one was open for 1% of the time, Pallas kernels for 5%

profile of v1, /device:TPU:1, one launch (start us, length us, event | category | flops | bytes accessed | tf_op | source)
XLA Modules:
  0.0 173.4 jit_solution(2054755589088569178)
XLA Ops:
  1.3 0.0 copy-start.1
  1.3 0.7 copy-done.1
  2.0 0.7 copy-done.3
  2.6 0.9 copy-done.7
  3.5 0.9 copy-done.8
  4.4 1.7 shard_map.146
  6.1 20.4 %all-to-all-start = ((bf16[128,24,128]{2,1,0:T(8,128)(2,1)}), bf16[128,24,128]{2,1,0:T(8,128)(2,1)S(1)}, u32[]{:S(2)}, u32[]{:S(2)}) async-start(bf16[128,24,128]{2,1,0:T(8,128)(2,1)} %bitcast.3), calls=%async_computation | async-start | bytes 1572864 | tf_op jit(solution)/shard_map/all_to_all | solution.py:300
  26.5 2.9 %shard_map.149.own_hbm = bf16[1024,768]{1,0:T(8,128)(2,1)} custom-call(f32[4,6]{1,0:T(4,128)} %gs_ref.1, f32[4,6]{1,0:T(4,128)} %us_ref.1, bf16[512,768]{1,0:T(8,128)(2,1)} %gc_ref.1, bf16[512,768]{1,0:T(8,128)(2,1)} %uc_ref.1), custom_call_target="tpu_custom_call" | custom-call | flops 786432 | bytes 3145728 | tf_op jit(solution)/shard_map/pallas_call | solution.py:32
  29.4 3.3 %collective-permute-start.2 = (bf16[1024,768]{1,0:T(8,128)(2,1)}, bf16[1024,768]{1,0:T(8,128)(2,1)S(1)}, u32[]{:S(2)}, u32[]{:S(2)}) collective-permute-start(bf16[1024,768]{1,0:T(8,128)(2,1)} %shard_map.149.own_hbm), channel_id=1, source_target_pairs={{0,128},{128,256},{256,384},{384,0},{1,129},{129,257},{257,385},{3... | collective-permute-start | bytes 4718600 | tf_op jit(solution)/shard_map/ppermute | solution.py:278
  32.7 3.4 %collective-permute-start = (bf16[1024,768]{1,0:T(8,128)(2,1)}, bf16[1024,768]{1,0:T(8,128)(2,1)S(1)}, u32[]{:S(2)}, u32[]{:S(2)}) collective-permute-start(bf16[1024,768]{1,0:T(8,128)(2,1)} %shard_map.149.own_hbm), channel_id=1, source_target_pairs={{0,384},{128,0},{256,128},{384,256},{1,385},{129,1},{257,129},{385... | collective-permute-start | bytes 4718600 | tf_op jit(solution)/shard_map/ppermute | solution.py:278
  36.1 31.9 %collective-permute-done.2.prev_hbm = bf16[1024,768]{1,0:T(8,128)(2,1)S(1)} collective-permute-done((bf16[1024,768]{1,0:T(8,128)(2,1)}, bf16[1024,768]{1,0:T(8,128)(2,1)S(1)}, u32[]{:S(2)}, u32[]{:S(2)}) %collective-permute-start.2) | collective-permute-done | bytes 1572896 | tf_op jit(solution)/shard_map/ppermute | solution.py:278
  68.0 0.1 slice.9
  68.1 1.9 %collective-permute-start.3 = (bf16[512,768]{1,0:T(8,128)(2,1)S(1)}, bf16[512,768]{1,0:T(8,128)(2,1)S(1)}, u32[]{:S(2)}, u32[]{:S(2)}) collective-permute-start(bf16[512,768]{1,0:T(8,128)(2,1)S(1)} %slice.9), channel_id=1, source_target_pairs={{0,128},{128,256},{256,384},{384,0},{1,129},{129,257},{257,385},{3... | collective-permute-start | bytes 2359304 | tf_op jit(solution)/shard_map/ppermute | solution.py:278
  70.0 0.0 collective-permute-done.next_hbm
  70.0 0.0 copy-start.10
  70.0 1.0 slice.8
  71.0 0.0 copy-done.9
  71.0 0.4 copy-done.10
  71.5 4.6 %collective-permute-start.1 = (bf16[512,768]{1,0:T(8,128)(2,1)}, bf16[512,768]{1,0:T(8,128)(2,1)}, u32[]{:S(2)}, u32[]{:S(2)}) collective-permute-start(bf16[512,768]{1,0:T(8,128)(2,1)} %slice.8), channel_id=1, source_target_pairs={{0,384},{128,0},{256,128},{384,256},{1,385},{129,1},{257,129},{385... | collective-permute-start | bytes 2359304 | tf_op jit(solution)/shard_map/ppermute | solution.py:278
  76.0 0.0 copy-done.11
  76.0 0.1 copy.16.ds_ref
  76.1 1.1 copy-done
  77.3 0.8 shard_map.147.wd_ref
  78.0 0.0 all-to-all-done
  78.0 1.8 %shard_map.148 = bf16[4,96,1280]{2,1,0:T(8,128)(2,1)} custom-call(bf16[3072,128]{1,0:T(8,128)(2,1)S(1)} %bitcast.8, bf16[768,512]{1,0:T(8,128)(2,1)S(1)} %shard_map.147.wd_ref), custom_call_target="tpu_custom_call" | custom-call | flops 301989888 | bytes 2359296 | tf_op jit(solution)/shard_map/pallas_call | solution.py:32
  79.9 3.5 %all-to-all-start.1 = ((bf16[4,96,1280]{2,1,0:T(8,128)(2,1)}), bf16[4,96,1280]{2,1,0:T(8,128)(2,1)S(1)}, u32[]{:S(2)}, u32[]{:S(2)}) async-start(bf16[4,96,1280]{2,1,0:T(8,128)(2,1)} %shard_map.148), calls=%async_computation.1 | async-start | bytes 1966080 | tf_op jit(solution)/shard_map/all_to_all | solution.py:329
  83.4 5.2 %collective-permute-done.3.far_high_hbm = bf16[512,768]{1,0:T(8,128)(2,1)S(1)} collective-permute-done((bf16[512,768]{1,0:T(8,128)(2,1)S(1)}, bf16[512,768]{1,0:T(8,128)(2,1)S(1)}, u32[]{:S(2)}, u32[]{:S(2)}) %collective-permute-start.3) | collective-permute-done | bytes 786464 | tf_op jit(solution)/shard_map/ppermute | solution.py:278
  88.6 2.7 %collective-permute-done.1.far_low_hbm = bf16[512,768]{1,0:T(8,128)(2,1)} collective-permute-done((bf16[512,768]{1,0:T(8,128)(2,1)}, bf16[512,768]{1,0:T(8,128)(2,1)}, u32[]{:S(2)}, u32[]{:S(2)}) %collective-permute-start.1) | collective-permute-done | bytes 786464 | tf_op jit(solution)/shard_map/ppermute | solution.py:278
  91.3 7.7 %all-to-all-done.1.part_ref = bf16[4,96,1280]{2,1,0:T(8,128)(2,1)S(1)} async-done(((bf16[4,96,1280]{2,1,0:T(8,128)(2,1)}), bf16[4,96,1280]{2,1,0:T(8,128)(2,1)S(1)}, u32[]{:S(2)}, u32[]{:S(2)}) %all-to-all-start.1) | async-done | bytes 983072 | tf_op jit(solution)/shard_map/all_to_all | solution.py:329
  98.9 5.2 %shard_map.150 = (bf16[4,512,128]{2,1,0:T(8,128)(2,1)S(1)}, bf16[288,768]{1,0:T(8,128)(2,1)S(1)}) custom-call(s32[1]{0:T(128)} %bitcast.2.me_ref, bf16[4,96,1280]{2,1,0:T(8,128)(2,1)S(1)} %all-to-all-done.1.part_ref, bf16[1024,768]{1,0:T(8,128)(2,1)} %shard_map.149.own_hbm, bf16[1024,768]{1,0:T(8,128)(2,1)} %copy-done.10, ...), custom_call_target="tpu_custom_call" | custom-call | flops 1207959552 | bytes 6291456 | tf_op jit(solution)/shard_map/pallas_call | solution.py:32
  104.2 0.0 copy-start.5
  104.2 12.8 %all_to_all.20 = bf16[4,512,128]{2,1,0:T(8,128)(2,1)} all-to-all(bf16[4,512,128]{2,1,0:T(8,128)(2,1)S(1)} %get-tuple-element.18), channel_id=1, replica_groups=mesh['dp'=4,'expert'=128] {'dp'}, dimensions={0} | all-to-all | bytes 1048576 | tf_op jit(solution)/shard_map/all_to_all | solution.py:347
  117.0 0.0 copy-done.5
  117.0 22.0 %all-to-all-start.3 = ((bf16[128,16,128]{2,1,0:T(8,128)(2,1)}), bf16[128,16,128]{2,1,0:T(8,128)(2,1)S(1)}, u32[]{:S(2)}, u32[]{:S(2)}) async-start(bf16[128,16,128]{2,1,0:T(8,128)(2,1)} %bitcast.5), calls=%async_computation.3 | async-start | bytes 1048576 | tf_op jit(solution)/shard_map/all_to_all | solution.py:349
  139.0 0.0 copy-start.2
  139.0 0.0 copy-start.4
  139.0 2.8 %collective-permute-start.6 = (bf16[288,768]{1,0:T(8,128)(2,1)}, bf16[288,768]{1,0:T(8,128)(2,1)S(1)}, u32[]{:S(2)}, u32[]{:S(2)}) collective-permute-start(bf16[288,768]{1,0:T(8,128)(2,1)} %copy-done.5), channel_id=1, source_target_pairs={{0,384},{128,0},{256,128},{384,256},{1,385},{129,1},{257,129},{385... | collective-permute-start | bytes 1327112 | tf_op jit(solution)/shard_map/ppermute | solution.py:278
  141.8 3.1 %collective-permute-start.5 = (bf16[288,768]{1,0:T(8,128)(2,1)}, bf16[288,768]{1,0:T(8,128)(2,1)S(1)}, u32[]{:S(2)}, u32[]{:S(2)}) collective-permute-start(bf16[288,768]{1,0:T(8,128)(2,1)} %copy-done.5), channel_id=1, source_target_pairs={{0,256},{128,384},{256,0},{384,128},{1,257},{129,385},{257,1},{385... | collective-permute-start | bytes 1327112 | tf_op jit(solution)/shard_map/ppermute | solution.py:278
  144.9 1.9 %collective-permute-start.4 = (bf16[288,768]{1,0:T(8,128)(2,1)}, bf16[288,768]{1,0:T(8,128)(2,1)S(1)}, u32[]{:S(2)}, u32[]{:S(2)}) collective-permute-start(bf16[288,768]{1,0:T(8,128)(2,1)} %copy-done.5), channel_id=1, source_target_pairs={{0,128},{128,256},{256,384},{384,0},{1,129},{129,257},{257,385},{3... | collective-permute-start | bytes 1327112 | tf_op jit(solution)/shard_map/ppermute | solution.py:278
  146.9 5.1 %collective-permute-done.6.a3_ref = bf16[288,768]{1,0:T(8,128)(2,1)S(1)} collective-permute-done((bf16[288,768]{1,0:T(8,128)(2,1)}, bf16[288,768]{1,0:T(8,128)(2,1)S(1)}, u32[]{:S(2)}, u32[]{:S(2)}) %collective-permute-start.6) | collective-permute-done | bytes 442400 | tf_op jit(solution)/shard_map/ppermute | solution.py:278
  152.0 4.1 %collective-permute-done.5.a2_ref = bf16[288,768]{1,0:T(8,128)(2,1)S(1)} collective-permute-done((bf16[288,768]{1,0:T(8,128)(2,1)}, bf16[288,768]{1,0:T(8,128)(2,1)S(1)}, u32[]{:S(2)}, u32[]{:S(2)}) %collective-permute-start.5) | collective-permute-done | bytes 442400 | tf_op jit(solution)/shard_map/ppermute | solution.py:278
  156.1 11.0 %collective-permute-done.4.a1_ref = bf16[288,768]{1,0:T(8,128)(2,1)S(1)} collective-permute-done((bf16[288,768]{1,0:T(8,128)(2,1)}, bf16[288,768]{1,0:T(8,128)(2,1)S(1)}, u32[]{:S(2)}, u32[]{:S(2)}) %collective-permute-start.4) | collective-permute-done | bytes 442400 | tf_op jit(solution)/shard_map/ppermute | solution.py:278
  167.0 1.0 copy-done.6
  168.0 2.6 %shard_map.152 = (bf16[512,768]{1,0:T(8,128)(2,1)}, bf16[512,768]{1,0:T(8,128)(2,1)}, bf16[768,512]{1,0:T(8,128)(2,1)}) custom-call(s32[1]{0:T(128)} %bitcast.2.me_ref, bf16[3072,128]{1,0:T(8,128)(2,1)S(1)} %bitcast.9, bf16[288,768]{1,0:T(8,128)(2,1)S(1)} %copy-done.6, bf16[288,768]{1,0:T(8,128)(2,1)S(1)} %collective-permute-done.4.a1_ref, ...), custom_call_target="tpu_custom_call" | custom-call | flops 905969664 | bytes 4718592 | tf_op jit(solution)/shard_map/pallas_call | solution.py:32
  170.7 1.6 all-to-all-done.3
  172.2 0.0 copy-done.2
  172.2 0.0 copy-done.4
  172.2 1.2 shard_map.151
  (7 shorter events, 0.0 us)
Async XLA Ops:
  1.3 0.7 copy-start.1
  2.0 0.7 copy-start.3
  2.6 0.9 copy-start.7
  3.5 0.9 copy-start.8
  6.1 71.9 %all-to-all-start = ((bf16[128,24,128]{2,1,0:T(8,128)(2,1)}), bf16[128,24,128]{2,1,0:T(8,128)(2,1)S(1)}, u32[]{:S(2)}, u32[]{:S(2)}) async-start(bf16[128,24,128]{2,1,0:T(8,128)(2,1)} %bitcast.3), calls=%async_computation | async-start | bytes 1572864 | tf_op jit(solution)/shard_map/all_to_all | solution.py:300
  29.4 46.7 %copy-start.11 = (f32[6,4]{0,1:T(4,128)S(1)}, f32[6,4]{0,1:T(4,128)}, u32[]{:S(2)}) copy-start(f32[6,4]{0,1:T(4,128)} %param.20) | copy-start | bytes 292
  29.4 38.6 %collective-permute-start.2 = (bf16[1024,768]{1,0:T(8,128)(2,1)}, bf16[1024,768]{1,0:T(8,128)(2,1)S(1)}, u32[]{:S(2)}, u32[]{:S(2)}) collective-permute-start(bf16[1024,768]{1,0:T(8,128)(2,1)} %shard_map.149.own_hbm), channel_id=1, source_target_pairs={{0,128},{128,256},{256,384},{384,0},{1,129},{129,257},{257,385},{3... | collective-permute-start | bytes 4718600 | tf_op jit(solution)/shard_map/ppermute | solution.py:278
  32.7 37.3 %collective-permute-start = (bf16[1024,768]{1,0:T(8,128)(2,1)}, bf16[1024,768]{1,0:T(8,128)(2,1)S(1)}, u32[]{:S(2)}, u32[]{:S(2)}) collective-permute-start(bf16[1024,768]{1,0:T(8,128)(2,1)} %shard_map.149.own_hbm), channel_id=1, source_target_pairs={{0,384},{128,0},{256,128},{384,256},{1,385},{129,1},{257,129},{385... | collective-permute-start | bytes 4718600 | tf_op jit(solution)/shard_map/ppermute | solution.py:278
  68.0 3.0 %copy-start.9 = (bf16[1024,768]{1,0:T(8,128)(2,1)}, bf16[1024,768]{1,0:T(8,128)(2,1)S(1)}, u32[]{:S(2)}) copy-start(bf16[1024,768]{1,0:T(8,128)(2,1)S(1)} %collective-permute-done.2.prev_hbm) | copy-start | bytes 4718596
  68.1 20.5 %collective-permute-start.3 = (bf16[512,768]{1,0:T(8,128)(2,1)S(1)}, bf16[512,768]{1,0:T(8,128)(2,1)S(1)}, u32[]{:S(2)}, u32[]{:S(2)}) collective-permute-start(bf16[512,768]{1,0:T(8,128)(2,1)S(1)} %slice.9), channel_id=1, source_target_pairs={{0,128},{128,256},{256,384},{384,0},{1,129},{129,257},{257,385},{3... | collective-permute-start | bytes 2359304 | tf_op jit(solution)/shard_map/ppermute | solution.py:278
  70.0 1.5 copy-start.10
  71.5 19.8 %collective-permute-start.1 = (bf16[512,768]{1,0:T(8,128)(2,1)}, bf16[512,768]{1,0:T(8,128)(2,1)}, u32[]{:S(2)}, u32[]{:S(2)}) collective-permute-start(bf16[512,768]{1,0:T(8,128)(2,1)} %slice.8), channel_id=1, source_target_pairs={{0,384},{128,0},{256,128},{384,256},{1,385},{129,1},{257,129},{385... | collective-permute-start | bytes 2359304 | tf_op jit(solution)/shard_map/ppermute | solution.py:278
  76.1 1.1 copy-start
  79.9 19.1 %all-to-all-start.1 = ((bf16[4,96,1280]{2,1,0:T(8,128)(2,1)}), bf16[4,96,1280]{2,1,0:T(8,128)(2,1)S(1)}, u32[]{:S(2)}, u32[]{:S(2)}) async-start(bf16[4,96,1280]{2,1,0:T(8,128)(2,1)} %shard_map.148), calls=%async_computation.1 | async-start | bytes 1966080 | tf_op jit(solution)/shard_map/all_to_all | solution.py:329
  104.2 12.8 %copy-start.5 = (bf16[288,768]{1,0:T(8,128)(2,1)}, bf16[288,768]{1,0:T(8,128)(2,1)S(1)}, u32[]{:S(2)}) copy-start(bf16[288,768]{1,0:T(8,128)(2,1)S(1)} %get-tuple-element.23.a0_ref) | copy-start | bytes 1327108
  117.0 55.2 %all-to-all-start.3 = ((bf16[128,16,128]{2,1,0:T(8,128)(2,1)}), bf16[128,16,128]{2,1,0:T(8,128)(2,1)S(1)}, u32[]{:S(2)}, u32[]{:S(2)}) async-start(bf16[128,16,128]{2,1,0:T(8,128)(2,1)} %bitcast.5), calls=%async_computation.3 | async-start | bytes 1048576 | tf_op jit(solution)/shard_map/all_to_all | solution.py:349
  139.0 33.2 %copy-start.2 = (s32[128,2]{0,1:T(2,128)S(1)}, s32[128,2]{0,1:T(2,128)}, u32[]{:S(2)}) copy-start(s32[128,2]{0,1:T(2,128)} %param.12) | copy-start | bytes 3076
  139.0 33.2 %copy-start.4 = (f32[128,2]{0,1:T(2,128)S(1)}, f32[128,2]{0,1:T(2,128)}, u32[]{:S(2)}) copy-start(f32[128,2]{0,1:T(2,128)} %param.13) | copy-start | bytes 3076
  139.0 12.9 %collective-permute-start.6 = (bf16[288,768]{1,0:T(8,128)(2,1)}, bf16[288,768]{1,0:T(8,128)(2,1)S(1)}, u32[]{:S(2)}, u32[]{:S(2)}) collective-permute-start(bf16[288,768]{1,0:T(8,128)(2,1)} %copy-done.5), channel_id=1, source_target_pairs={{0,384},{128,0},{256,128},{384,256},{1,385},{129,1},{257,129},{385... | collective-permute-start | bytes 1327112 | tf_op jit(solution)/shard_map/ppermute | solution.py:278
  141.8 14.2 %collective-permute-start.5 = (bf16[288,768]{1,0:T(8,128)(2,1)}, bf16[288,768]{1,0:T(8,128)(2,1)S(1)}, u32[]{:S(2)}, u32[]{:S(2)}) collective-permute-start(bf16[288,768]{1,0:T(8,128)(2,1)} %copy-done.5), channel_id=1, source_target_pairs={{0,256},{128,384},{256,0},{384,128},{1,257},{129,385},{257,1},{385... | collective-permute-start | bytes 1327112 | tf_op jit(solution)/shard_map/ppermute | solution.py:278
  144.9 22.1 %collective-permute-start.4 = (bf16[288,768]{1,0:T(8,128)(2,1)}, bf16[288,768]{1,0:T(8,128)(2,1)S(1)}, u32[]{:S(2)}, u32[]{:S(2)}) collective-permute-start(bf16[288,768]{1,0:T(8,128)(2,1)} %copy-done.5), channel_id=1, source_target_pairs={{0,128},{128,256},{256,384},{384,0},{1,129},{129,257},{257,385},{3... | collective-permute-start | bytes 1327112 | tf_op jit(solution)/shard_map/ppermute | solution.py:278
  167.0 1.0 copy-start.6
